TPU v7x, 32 devices: a whole 2x2x4 slice. The times are simulated.
32 devices in a mesh: dp: 8 (over y, x, core), head: 4 (over z).
Axes of the slice: x: 2, y: 2, z: 4, core: 2. Of those that a mesh axis runs over, the one named last changes fastest.
Arguments:
- tokens: bfloat16 [2048, 2048], P('dp'), may hold values from -6 to 6
- weights: bfloat16 [4, 768, 2048], P('head', 'dp'), may hold values from -0.13479223 to 0.13479223, as said below
- query_gain: float32 [128], replicated, may hold values from 0.25 to 1.75
- key_gain: float32 [128], replicated, may hold values from 0.25 to 1.75
- first_row: int32 [2048], P('dp'), may hold values from 0 to 2047, as said below
- cotangent: bfloat16 [2048, 2048], P('dp', 'head'), may hold values from -6 to 6
Outputs:
- attended: bfloat16 [2048, 2048], P('dp', 'head')
- token_grad: bfloat16 [2048, 2048], P('dp', 'head')
- weight_grad: float32 [4, 768, 2048], P('head', 'dp')
Inputs may be any that keep to these rules, and one draw needn't show every extreme that they name: first_row[i] is the position of the first row of row i's document: documents are runs of consecutive rows, each at most 512 rows long, one of exactly 512 rows, and the last row begins a document of its own. For every even g, weights[g] and weights[g + 1] are equal in their last 256 rows: each key-value head is held by two head devices.
All inputs are finite; a program needn't handle non-finite values.
Results may differ from a plain program's by a relative error of at most 0.017.
Values may be sent and summed in bfloat16 or wider, within the bound.
No kernel may reach another device: no remote copies, remote signals or barrier semaphores. Data moves between devices by JAX's collectives and lax.ppermute only.
A program may use at most 64 MiB of HBM per device.

v0:
```python
import math
import jax
import jax.numpy as jnp
from jax import lax
from jax.sharding import PartitionSpec as P

HD = 128
QH_DEV = 4
COLS = 768
ROWS = 256
SPAN = 2
EPSILON = 1e-06
THETA = 1000000.0
STRETCH = 0.25


def from_behind(x, axis, by):
    devices = lax.axis_size(axis)
    pairs = [(i, i + by) for i in range(devices) if 0 <= i + by < devices]
    return lax.ppermute(x, axis, pairs)


def partner(x, axis, apart):
    return lax.ppermute(x, axis, [(i, i ^ 1 << apart) for i in range(lax.axis_size(axis))])


def rope_tables(position, head_size):
    middle = head_size // 2
    channel = jnp.arange(middle, dtype=jnp.float32)
    frequency = THETA ** (-2.0 * channel / head_size)
    angles = (position.astype(jnp.float32) * STRETCH)[:, None] * frequency[None, :]
    angles = jnp.concatenate([angles, angles], axis=1)
    return (jnp.cos(angles), jnp.sin(angles))


def normalize_rotate(values, scaling, cosine_table, sine_table):
    factor = lax.rsqrt(jnp.mean(values * values, axis=-1, keepdims=True) + EPSILON)
    normed = values * factor * scaling
    middle = normed.shape[-1] // 2
    turned = jnp.concatenate([-normed[..., middle:], normed[..., :middle]], axis=-1)
    return normed * cosine_table + turned * sine_table


def prepare(projected, query_gain, key_gain, cosine_table, sine_table):
    row_count = projected.shape[0]
    queries = projected[:, : QH_DEV * HD].reshape(row_count, QH_DEV, HD)
    queries = normalize_rotate(
        queries, query_gain, cosine_table[:, None, :], sine_table[:, None, :]
    )
    key_part = normalize_rotate(
        projected[:, QH_DEV * HD : (QH_DEV + 1) * HD], key_gain, cosine_table, sine_table
    )
    value_part = projected[:, (QH_DEV + 1) * HD :]
    return (queries, key_part, value_part)


def attend_window(queries, window, upstream, first_rows, query_place, key_place):
    score_scale = 1.0 / math.sqrt(HD)
    key_window = window[:, :HD]
    value_window = window[:, HD:]
    visible = (key_place[None, :] >= first_rows[:, None]) & (
        key_place[None, :] <= query_place[:, None]
    )
    score = (
        jnp.einsum("rhc,kc->rhk", queries, key_window, preferred_element_type=jnp.float32)
        * score_scale
    )
    weight = jnp.where(visible[:, None, :], jnp.exp(score), 0.0)
    denominator = jnp.sum(weight, axis=-1)
    summed = jnp.einsum(
        "rhk,kc->rhc", weight.astype(jnp.bfloat16), value_window, preferred_element_type=jnp.float32
    )
    attended = (summed / denominator[..., None]).astype(jnp.bfloat16)
    probability = weight / denominator[..., None]
    row_delta = jnp.sum(upstream.astype(jnp.float32) * attended.astype(jnp.float32), axis=-1)
    grad_prob = jnp.einsum(
        "rhc,kc->rhk", upstream, value_window, preferred_element_type=jnp.float32
    )
    grad_score = (probability * (grad_prob - row_delta[..., None]) * score_scale).astype(
        jnp.bfloat16
    )
    grad_query = jnp.einsum(
        "rhk,kc->rhc", grad_score, key_window, preferred_element_type=jnp.float32
    )
    grad_key = jnp.einsum("rhk,rhc->kc", grad_score, queries, preferred_element_type=jnp.float32)
    grad_value = jnp.einsum(
        "rhk,rhc->kc",
        probability.astype(jnp.bfloat16),
        upstream,
        preferred_element_type=jnp.float32,
    )
    return (attended, grad_query, jnp.concatenate([grad_key, grad_value], axis=1))


def body(tokens, weights, query_gain, key_gain, first_row, cotangent):
    block_index = lax.axis_index("dp")
    position = block_index * ROWS + jnp.arange(ROWS, dtype=jnp.int32)
    key_place = (block_index - SPAN) * ROWS + jnp.arange((SPAN + 1) * ROWS, dtype=jnp.int32)
    cosine_table, sine_table = rope_tables(position, HD)
    weight_piece = lax.all_gather(weights, "dp", axis=1, tiled=True)
    projected = jnp.einsum("rd,cd->rc", tokens, weight_piece[0], preferred_element_type=jnp.float32)
    prepared, pullback = jax.vjp(
        lambda values: prepare(values, query_gain, key_gain, cosine_table, sine_table), projected
    )
    queries = prepared[0].astype(jnp.bfloat16)
    key_value = jnp.concatenate([prepared[1], prepared[2]], axis=1).astype(jnp.bfloat16)
    earlier = [from_behind(key_value, "dp", distance) for distance in range(SPAN, 0, -1)]
    window = jnp.concatenate(earlier + [key_value], axis=0)
    upstream = cotangent.reshape(ROWS, QH_DEV, HD)
    attended, grad_query, slot_grads = attend_window(
        queries, window, upstream, first_row, position, key_place
    )
    pair_grad = slot_grads[SPAN * ROWS :]
    for distance in range(1, SPAN + 1):
        slot_index = SPAN - distance
        pair_grad = pair_grad + from_behind(
            slot_grads[slot_index * ROWS : (slot_index + 1) * ROWS].astype(jnp.bfloat16),
            "dp",
            -distance,
        ).astype(jnp.float32)
    grad_projected = pullback((grad_query, pair_grad[:, :HD], pair_grad[:, HD:]))[0].astype(
        jnp.bfloat16
    )
    partial_grad = jnp.dot(grad_projected, weight_piece[0], preferred_element_type=jnp.float32)
    token_grad = lax.psum_scatter(
        partial_grad.astype(jnp.bfloat16), "head", scatter_dimension=1, tiled=True
    )
    shard_rows = COLS // lax.axis_size("dp")
    own_grad = lax.psum_scatter(
        jnp.einsum("rc,rd->cd", grad_projected, tokens, preferred_element_type=jnp.float32),
        "dp",
        scatter_dimension=0,
        tiled=True,
    )
    partner_grad = partner(own_grad.astype(jnp.bfloat16), "head", 0).astype(own_grad.dtype)
    global_rows = block_index * shard_rows + jnp.arange(shard_rows, dtype=jnp.int32)
    shared_rows = global_rows >= QH_DEV * HD
    weight_grad = jnp.where(shared_rows[:, None], own_grad + partner_grad, own_grad)
    return (attended.reshape(ROWS, QH_DEV * HD), token_grad, weight_grad[None])


def solution(mesh):
    in_specs = (P("dp", None), P("head", "dp", None), P(), P(), P("dp"), P("dp", "head"))
    out_specs = (P("dp", "head"), P("dp", "head"), P("head", "dp", None))
    return jax.shard_map(body, mesh=mesh, in_specs=in_specs, out_specs=out_specs, check_vma=False)
```

profile of v0, /device:TPU:0, one launch (start us, length us, event | category | flops | bytes accessed | tf_op | source)
XLA Modules:
  0.0 185.5 jit_solution(12164193166599489742)
XLA Ops:
  7.2 0.7 all-gather.2.cloned.1.call-update
  8.0 1.8 copy.66
  9.9 1.6 compare_and_fusion
  11.5 33.3 %all-gather.2.cloned.1.call-done = bf16[1,768,2048]{2,1,0:T(8,128)(2,1)} async-done(((bf16[1,96,2048]{2,1,0:T(8,128)(2,1)}), bf16[1,768,2048]{2,1,0:T(8,128)(2,1)}) %all-gather.2.cloned.1.call-update) | async-done | bytes 3145744 | tf_op jit(solution)/shard_map/all_gather | solution.py:100
  44.8 2.9 %fusion.4 = f32[256,768]{1,0:T(8,128)S(1)} fusion(bf16[256,2048]{1,0:T(8,128)(2,1)S(1)} %copy-done, bf16[1,768,2048]{2,1,0:T(8,128)(2,1)} %all-gather.2.cloned.1.call-done), kind=kOutput, calls=%fused_computation.5 | convolution fusion | flops 805306368 | bytes 4980736 | tf_op jit(solution)/shard_map/rd,cd->rc/dot_general | solution.py:101
  48.1 1.3 fusion.39
  49.4 0.7 pad_maximum_fusion.2
  50.0 2.8 %collective-permute-start.1 = (bf16[256,256]{1,0:T(8,128)(2,1)}, bf16[256,256]{1,0:T(8,128)(2,1)}, u32[]{:S(2)}, u32[]{:S(2)}) collective-permute-start(bf16[256,256]{1,0:T(8,128)(2,1)} %pad_maximum_fusion.2), channel_id=1, source_target_pairs={{0,4},{4,8},{8,12},{12,16},{16,20},{20,24},{24,28},{1,5},{5,9},{9,... | collective-permute-start | bytes 393224 | tf_op jit(solution)/shard_map/ppermute | solution.py:20
  52.8 3.4 %collective-permute-start = (bf16[256,256]{1,0:T(8,128)(2,1)}, bf16[256,256]{1,0:T(8,128)(2,1)}, u32[]{:S(2)}, u32[]{:S(2)}) collective-permute-start(bf16[256,256]{1,0:T(8,128)(2,1)} %pad_maximum_fusion.2), channel_id=1, source_target_pairs={{0,8},{4,12},{8,16},{12,20},{16,24},{20,28},{1,9},{5,13},{9,17},{1... | collective-permute-start | bytes 393224 | tf_op jit(solution)/shard_map/ppermute | solution.py:20
  57.0 1.0 copy.63
  58.6 0.9 collective-permute-done
  59.5 1.0 maximum_maximum_fusion
  60.5 1.0 fusion.10
  61.6 1.4 multiply_reduce_fusion.1
  63.0 1.1 fusion.19
  64.1 1.5 fusion.1
  66.2 0.7 broadcast_multiply_fusion
  67.1 0.7 fusion.50
  67.8 1.3 collective-permute-start.2
  69.1 1.3 collective-permute-start.3
  71.4 7.2 %collective-permute-done.3 = bf16[256,256]{1,0:T(8,128)(2,1)} collective-permute-done((bf16[256,256]{1,0:T(8,128)(2,1)}, bf16[256,256]{1,0:T(8,128)(2,1)}, u32[]{:S(2)}, u32[]{:S(2)}) %collective-permute-start.3) | collective-permute-done | bytes 131104 | tf_op jit(solution)/shard_map/ppermute | solution.py:20
  78.6 1.1 fusion.35
  80.3 0.6 multiply_reduce_fusion.3
  81.1 3.7 %fusion.48 = f32[768,2048]{1,0:T(8,128)} fusion(bf16[256,2048]{1,0:T(8,128)(2,1)S(1)} %copy-done, f32[256,512]{1,0:T(8,128)S(1)} %copy.87, f32[256,128]{1,0:T(8,128)S(1)} %add_add_fusion.1, f32[256,128]{1,0:T(8,128)S(1)} %get-tuple-element.23), kind=kOutput, calls=%fused_computation.82 | convolution fusion | flops 805896192 | bytes 8126464 | tf_op jit(solution)/shard_map/rc,rd->cd/dot_general | solution.py:130
  84.9 3.9 %fusion.6 = bf16[256,2048]{1,0:T(8,128)(2,1)} fusion(bf16[1,768,2048]{2,1,0:T(8,128)(2,1)} %all-gather.2.cloned.1.call-done, f32[256,512]{1,0:T(8,128)S(1)} %copy.87, f32[256,128]{1,0:T(8,128)S(1)} %add_add_fusion.1, f32[256,128]{1,0:T(8,128)S(1)} %get-tuple-element.23), kind=kOutput, calls=%fused_computation.8 | convolution fusion | flops 806420480 | bytes 4980736 | tf_op jit(solution)/shard_map/dot_general | solution.py:124
  88.8 59.1 %reduce-scatter.5.cloned.1.call-done = f32[96,2048]{1,0:T(8,128)} async-done(((f32[768,2048]{1,0:T(8,128)}), f32[96,2048]{1,0:T(8,128)}) %reduce-scatter.5.cloned.1.call-update) | async-done | bytes 786448 | tf_op jit(solution)/shard_map/reduce_scatter | solution.py:129
  147.9 1.2 convert_element_type.61
  149.1 1.6 collective-permute-start.4
  150.6 0.8 copy.75
  151.5 11.0 %collective-permute-done.4 = bf16[96,2048]{1,0:T(8,128)(2,1)S(1)} collective-permute-done((bf16[96,2048]{1,0:T(8,128)(2,1)S(1)}, bf16[96,2048]{1,0:T(8,128)(2,1)S(1)}, u32[]{:S(2)}, u32[]{:S(2)}) %collective-permute-start.4) | collective-permute-done | bytes 393248 | tf_op jit(solution)/shard_map/ppermute | solution.py:24
  162.5 2.2 %fusion.29 = f32[1,96,2048]{2,1,0:T(8,128)} fusion(f32[96,2048]{1,0:T(8,128)} %reduce-scatter.5.cloned.1.call-done, bf16[96,2048]{1,0:T(8,128)(2,1)S(1)} %collective-permute-done.4, pred[96]{0:T(512)(128)(4,1)S(1)} %add_compare_fusion), kind=kLoop, calls=%fused_computation.27 | loop fusion | flops 589824 | bytes 1966176 | tf_op jit(solution)/shard_map/broadcast_in_dim | solution.py:139
  164.7 14.3 %reduce-scatter.3.cloned.1.call-done = bf16[256,512]{1,0:T(8,128)(2,1)} async-done(((bf16[256,2048]{1,0:T(8,128)(2,1)}), bf16[256,512]{1,0:T(8,128)(2,1)}) %reduce-scatter.3.cloned.1.call-update) | async-done | bytes 262160 | tf_op jit(solution)/shard_map/reduce_scatter | solution.py:125
  (53 shorter events, 4.5 us)
Async XLA Ops:
  7.2 37.7 %copy-start = (bf16[256,2048]{1,0:T(8,128)(2,1)S(1)}, bf16[256,2048]{1,0:T(8,128)(2,1)}, u32[]{:S(2)}) copy-start(bf16[256,2048]{1,0:T(8,128)(2,1)} %param.6) | copy-start | bytes 3145732
  7.2 37.6 %all-gather.2.cloned.1.call-start = ((), (), s32[]{:S(2)}) async-start(), calls=%async_computation.2 | async-start | bytes 3538944 | tf_op jit(solution)/shard_map/all_gather | solution.py:100
  7.9 140.0 %reduce-scatter.5.cloned.1.call-start = ((), (), s32[]{:S(2)}) async-start(), calls=%async_computation.4 | async-start | bytes 7077888 | tf_op jit(solution)/shard_map/reduce_scatter | solution.py:129
  9.8 38.1 %copy-start.6 = (f32[128]{0:T(128)S(1)}, f32[128]{0:T(128)}, u32[]{:S(2)}) copy-start(f32[128]{0:T(128)} %param.9) | copy-start | bytes 1540
  47.9 10.4 %copy-start.5 = (f32[128]{0:T(128)S(1)}, f32[128]{0:T(128)}, u32[]{:S(2)}) copy-start(f32[128]{0:T(128)} %param.8) | copy-start | bytes 1540
  50.0 8.5 %collective-permute-start.1 = (bf16[256,256]{1,0:T(8,128)(2,1)}, bf16[256,256]{1,0:T(8,128)(2,1)}, u32[]{:S(2)}, u32[]{:S(2)}) collective-permute-start(bf16[256,256]{1,0:T(8,128)(2,1)} %pad_maximum_fusion.2), channel_id=1, source_target_pairs={{0,4},{4,8},{8,12},{12,16},{16,20},{20,24},{24,28},{1,5},{5,9},{9,... | collective-permute-start | bytes 393224 | tf_op jit(solution)/shard_map/ppermute | solution.py:20
  52.8 6.7 %collective-permute-start = (bf16[256,256]{1,0:T(8,128)(2,1)}, bf16[256,256]{1,0:T(8,128)(2,1)}, u32[]{:S(2)}, u32[]{:S(2)}) collective-permute-start(bf16[256,256]{1,0:T(8,128)(2,1)} %pad_maximum_fusion.2), channel_id=1, source_target_pairs={{0,8},{4,12},{8,16},{12,20},{16,24},{20,28},{1,9},{5,13},{9,17},{1... | collective-permute-start | bytes 393224 | tf_op jit(solution)/shard_map/ppermute | solution.py:20
  58.2 2.3 %copy-start.4 = (pred[256,768]{1,0:T(8,128)(4,1)S(1)}, pred[256,768]{1,0:T(8,128)(4,1)}, u32[]{:S(2)}) copy-start(pred[256,768]{1,0:T(8,128)(4,1)} %compare_and_fusion) | copy-start | bytes 589828
  58.4 3.1 %copy-start.3 = (bf16[256,512]{0,1:T(8,128)(2,1)S(1)}, bf16[256,512]{0,1:T(8,128)(2,1)}, u32[]{:S(2)}) copy-start(bf16[256,512]{0,1:T(8,128)(2,1)} %copy.66) | copy-start | bytes 786436
  64.1 3.0 %copy-start.1 = (f32[768,128]{1,0:T(8,128)}, f32[768,128]{1,0:T(8,128)S(1)}, u32[]{:S(2)}) copy-start(f32[768,128]{1,0:T(8,128)S(1)} %fusion.19) | copy-start | bytes 1179652
  67.8 3.6 %collective-permute-start.2 = (bf16[256,256]{1,0:T(8,128)(2,1)}, bf16[256,256]{1,0:T(8,128)(2,1)}, u32[]{:S(2)}, u32[]{:S(2)}) collective-permute-start(bf16[256,256]{1,0:T(8,128)(2,1)} %get-tuple-element.21), channel_id=1, source_target_pairs={{4,0},{8,4},{12,8},{16,12},{20,16},{24,20},{28,24},{5,1},{9,5},{13... | collective-permute-start | bytes 393224 | tf_op jit(solution)/shard_map/ppermute | solution.py:20
  69.1 9.5 %collective-permute-start.3 = (bf16[256,256]{1,0:T(8,128)(2,1)}, bf16[256,256]{1,0:T(8,128)(2,1)}, u32[]{:S(2)}, u32[]{:S(2)}) collective-permute-start(bf16[256,256]{1,0:T(8,128)(2,1)} %get-tuple-element.22), channel_id=1, source_target_pairs={{8,0},{12,4},{16,8},{20,12},{24,16},{28,20},{9,1},{13,5},{17,9},{2... | collective-permute-start | bytes 393224 | tf_op jit(solution)/shard_map/ppermute | solution.py:20
  84.8 65.8 %copy-start.2 = (bf16[256,4,128]{0,2,1:T(8,128)(2,1)S(1)}, bf16[256,4,128]{0,2,1:T(8,128)(2,1)}, u32[]{:S(2)}) copy-start(bf16[256,4,128]{0,2,1:T(8,128)(2,1)} %get-tuple-element.35) | copy-start | bytes 786436
  84.8 94.1 %reduce-scatter.3.cloned.1.call-start = ((), (), s32[]{:S(2)}) async-start(), calls=%async_computation.3 | async-start | bytes 1310720 | tf_op jit(solution)/shard_map/reduce_scatter | solution.py:125
  149.1 13.5 %collective-permute-start.4 = (bf16[96,2048]{1,0:T(8,128)(2,1)S(1)}, bf16[96,2048]{1,0:T(8,128)(2,1)S(1)}, u32[]{:S(2)}, u32[]{:S(2)}) collective-permute-start(bf16[96,2048]{1,0:T(8,128)(2,1)S(1)} %convert_element_type.61), channel_id=1, source_target_pairs={{0,1},{1,0},{2,3},{3,2},{4,5},{5,4},{6,7},{7,6},{8,9},{9,8},{10,11... | collective-permute-start | bytes 1179656 | tf_op jit(solution)/shard_map/ppermute | solution.py:24
Sparse Core Ops, SparseCore 0:
  9.9 34.8 all-gather.1
  84.9 62.8 reduce-scatter.4
  150.8 28.1 reduce-scatter.2
where the time goes:
time: 186 us
  waiting for transfers between devices  127 us (68%)
  matrix products  16.7 us (9%)
  between operations  14.1 us (8%)
  other arithmetic  11.9 us (6%)
  starting transfers between devices  10.4 us (6%)
  local copies, waits for them, and re-layouts  5.22 us (3%)
    reduce_scatter x1, waiting for transfers between devices, body(): lax.psum_scatter(jnp.einsum('rc,rd->cd', grad_projected, tokens, preferre...  59.1 us
    all_gather x1, waiting for transfers between devices, body(): weight_piece = lax.all_gather(weights, 'dp', axis=1, tiled=True)  33.3 us
    reduce_scatter x1, waiting for transfers between devices, body(): lax.psum_scatter(partial_grad.astype(jnp.bfloat16), 'head', scatter_dimen...  14.3 us
    ppermute x1, waiting for transfers between devices, partner(): lax.ppermute(x, axis, [(i, i ^ 1 << apart) for i in range(lax.axis_size(a...  11 us
    ppermute x4, starting transfers between devices, from_behind(): return lax.ppermute(x, axis, pairs)  8.74 us
    ppermute x4, waiting for transfers between devices, from_behind(): return lax.ppermute(x, axis, pairs)  8.71 us
    dot_general x1, matrix products, body(): jnp.dot(grad_projected, weight_piece[0], preferred_element_type=jnp.float32)  3.86 us
  transfers between devices with their start and end apart: 8, of which 7 were waited for; matrix products, arithmetic and copies ran while one was open for 8% of the time, Pallas kernels for 0%

commit v1 on v0

--- a/solution.py
+++ b/solution.py
@@ -3,6 +3,7 @@
 import jax.numpy as jnp
 from jax import lax
 from jax.sharding import PartitionSpec as P
+from jax.lax import axis_index, axis_size, ppermute
 
 HD = 128
 QH_DEV = 4
@@ -97,7 +98,19 @@
     position = block_index * ROWS + jnp.arange(ROWS, dtype=jnp.int32)
     key_place = (block_index - SPAN) * ROWS + jnp.arange((SPAN + 1) * ROWS, dtype=jnp.int32)
     cosine_table, sine_table = rope_tables(position, HD)
-    weight_piece = lax.all_gather(weights, "dp", axis=1, tiled=True)
+    wide_n = axis_size("dp")
+    store = tuple(((hop_no, (hop_no + 1) % wide_n) for hop_no in range(wide_n)))
+    in_order = tuple(((hop_no, (hop_no - 1) % wide_n) for hop_no in range(wide_n)))
+    tall, f_now = ([weights], [weights])
+    for _ in range(wide_n // 2):
+        arr_next = ppermute(tall[-1], "dp", store)
+        tall.append(arr_next)
+    for _ in range((wide_n - 1) // 2):
+        z1 = ppermute(f_now[-1], "dp", in_order)
+        f_now.append(z1)
+    val2 = jnp.concatenate([*tall[::-1], *f_now[1:]], axis=1)
+    after = axis_index("dp")
+    weight_piece = jnp.roll(val2, (after - wide_n // 2) * weights.shape[1], 1)
     projected = jnp.einsum("rd,cd->rc", tokens, weight_piece[0], preferred_element_type=jnp.float32)
     prepared, pullback = jax.vjp(
         lambda values: prepare(values, query_gain, key_gain, cosine_table, sine_table), projected

time: 186 us -> 192 us (1.032)
  starting transfers between devices: 10.4 us -> 19.5 us
  other arithmetic: 11.9 us -> 7.24 us
  local copies, waits for them, and re-layouts: 5.22 us -> 8.85 us
  matrix products: 16.7 us -> 13.9 us
    all_gather x1 -> x0, waiting for transfers between devices: 33.3 us -> none  [body(): weight_piece = lax.all_gather(weights, 'dp', axis=1, tiled=True)]
    ppermute x0 -> x7, waiting for transfers between devices: none -> 31.3 us  [the longest x4 31.3 us: body(): arr_next = ppermute(tall[-1], 'dp', store)]
    ppermute x0 -> x7, starting transfers between devices: none -> 8.58 us  [the longest x3 8.03 us: body(): z1 = ppermute(f_now[-1], 'dp', in_order)]
    unnamed x16 -> x27, local copies, waits for them, and re-layouts: 2.68 us -> 8.79 us
  transfers between devices with their start and end apart: 8 -> 14, of which waited for: 7 -> 9; matrix products, arithmetic and copies ran while one was open for 8% -> 7% of each run, Pallas kernels for 0% -> 0%
where the time goes in v1:
time: 192 us; the launch traced here: 191 us
  waiting for transfers between devices  127 us (66%)
  starting transfers between devices  19.5 us (10%)
  between operations  14.5 us (8%)
  matrix products  13.9 us (7%)
  local copies, waits for them, and re-layouts  8.85 us (5%)
  other arithmetic  7.24 us (4%)
    reduce_scatter x1, waiting for transfers between devices, body(): lax.psum_scatter(jnp.einsum('rc,rd->cd', grad_projected, tokens, preferre...  60.8 us
    ppermute x4, waiting for transfers between devices, body(): arr_next = ppermute(tall[-1], 'dp', store)  31.3 us
    reduce_scatter x1, waiting for transfers between devices, body(): lax.psum_scatter(partial_grad.astype(jnp.bfloat16), 'head', scatter_dimen...  14.2 us
    ppermute x1, waiting for transfers between devices, partner(): lax.ppermute(x, axis, [(i, i ^ 1 << apart) for i in range(lax.axis_size(a...  11.1 us
    ppermute x4, waiting for transfers between devices, from_behind(): return lax.ppermute(x, axis, pairs)  9.55 us
    ppermute x4, starting transfers between devices, from_behind(): return lax.ppermute(x, axis, pairs)  9.33 us
    unnamed x27, local copies, waits for them, and re-layouts  8.79 us
    ppermute x3, starting transfers between devices, body(): z1 = ppermute(f_now[-1], 'dp', in_order)  8.03 us
  transfers between devices with their start and end apart: 14, of which 9 were waited for; matrix products, arithmetic and copies ran while one was open for 7% of the time, Pallas kernels for 0%

profile of v1, /device:TPU:0, one launch (start us, length us, event | category | flops | bytes accessed | tf_op | source)
XLA Modules:
  0.0 191.1 jit_solution(8535409103176682693)
XLA Ops:
  7.8 8.5 %collective-permute-done = bf16[1,96,2048]{2,1,0:T(8,128)(2,1)S(1)} collective-permute-done((bf16[1,96,2048]{2,1,0:T(8,128)(2,1)}, bf16[1,96,2048]{2,1,0:T(8,128)(2,1)S(1)}, u32[]{:S(2)}, u32[]{:S(2)}) %collective-permute-start) | collective-permute-done | bytes 393248 | tf_op jit(solution)/shard_map/ppermute | solution.py:106
  16.3 2.6 %collective-permute-start.4 = (bf16[1,96,2048]{2,1,0:T(8,128)(2,1)}, bf16[1,96,2048]{2,1,0:T(8,128)(2,1)S(1)}, u32[]{:S(2)}, u32[]{:S(2)}) collective-permute-start(bf16[1,96,2048]{2,1,0:T(8,128)(2,1)} %param.7), channel_id=1, source_target_pairs={{0,28},{4,0},{8,4},{12,8},{16,12},{20,16},{24,20},{28,24},{1,29},{... | collective-permute-start | bytes 1179656 | tf_op jit(solution)/shard_map/ppermute | solution.py:109
  19.0 7.8 %collective-permute-done.1 = bf16[1,96,2048]{2,1,0:T(8,128)(2,1)S(1)} collective-permute-done((bf16[1,96,2048]{2,1,0:T(8,128)(2,1)S(1)}, bf16[1,96,2048]{2,1,0:T(8,128)(2,1)S(1)}, u32[]{:S(2)}, u32[]{:S(2)}) %collective-permute-start.1) | collective-permute-done | bytes 393248 | tf_op jit(solution)/shard_map/ppermute | solution.py:106
  26.8 2.7 %collective-permute-start.5 = (bf16[1,96,2048]{2,1,0:T(8,128)(2,1)S(1)}, bf16[1,96,2048]{2,1,0:T(8,128)(2,1)}, u32[]{:S(2)}, u32[]{:S(2)}) collective-permute-start(bf16[1,96,2048]{2,1,0:T(8,128)(2,1)S(1)} %collective-permute-done.4), channel_id=1, source_target_pairs={{0,28},{4,0},{8,4},{12,8},{16,12},{20,16},{24,20},{28,24},{1,29},{... | collective-permute-start | bytes 1179656 | tf_op jit(solution)/shard_map/ppermute | solution.py:109
  29.5 8.2 %collective-permute-done.2 = bf16[1,96,2048]{2,1,0:T(8,128)(2,1)S(1)} collective-permute-done((bf16[1,96,2048]{2,1,0:T(8,128)(2,1)S(1)}, bf16[1,96,2048]{2,1,0:T(8,128)(2,1)S(1)}, u32[]{:S(2)}, u32[]{:S(2)}) %collective-permute-start.2) | collective-permute-done | bytes 393248 | tf_op jit(solution)/shard_map/ppermute | solution.py:106
  37.7 1.1 copy.11
  38.9 0.9 compare_and_fusion
  39.8 2.7 %collective-permute-start.6 = (bf16[1,96,2048]{2,1,0:T(8,128)(2,1)}, bf16[1,96,2048]{2,1,0:T(8,128)(2,1)S(1)}, u32[]{:S(2)}, u32[]{:S(2)}) collective-permute-start(bf16[1,96,2048]{2,1,0:T(8,128)(2,1)} %collective-permute-done.5), channel_id=1, source_target_pairs={{0,28},{4,0},{8,4},{12,8},{16,12},{20,16},{24,20},{28,24},{1,29},{... | collective-permute-start | bytes 1179656 | tf_op jit(solution)/shard_map/ppermute | solution.py:109
  42.5 6.8 %collective-permute-done.3 = bf16[1,96,2048]{2,1,0:T(8,128)(2,1)} collective-permute-done((bf16[1,96,2048]{2,1,0:T(8,128)(2,1)S(1)}, bf16[1,96,2048]{2,1,0:T(8,128)(2,1)}, u32[]{:S(2)}, u32[]{:S(2)}) %collective-permute-start.3) | collective-permute-done | bytes 393248 | tf_op jit(solution)/shard_map/ppermute | solution.py:106
  49.2 1.0 constant_dynamic-update-slice_fusion.15
  50.4 1.0 constant_dynamic-update-slice_fusion.11
  51.4 1.0 constant_dynamic-update-slice_fusion.9
  52.5 1.0 constant_dynamic-update-slice_fusion.7
  53.7 1.0 constant_dynamic-update-slice_fusion.1
  54.8 1.0 fusion.21
  56.0 1.4 copy-done.2
  58.0 1.5 collective-permute-start.7
  59.5 5.3 %collective-permute-start.8 = (bf16[256,256]{0,1:T(8,128)(2,1)S(1)}, bf16[256,256]{0,1:T(8,128)(2,1)S(1)}, u32[]{:S(2)}, u32[]{:S(2)}) collective-permute-start(bf16[256,256]{0,1:T(8,128)(2,1)S(1)} %pad_maximum_fusion.2), channel_id=1, source_target_pairs={{0,4},{4,8},{8,12},{12,16},{16,20},{20,24},{24,28},{1,5},{5,9},{9,... | collective-permute-start | bytes 393224 | tf_op jit(solution)/shard_map/ppermute | solution.py:21
  65.8 1.0 fusion.12
  67.6 1.0 fusion.24
  68.6 1.4 fusion.1
  71.1 1.3 collective-permute-start.10
  72.4 1.3 collective-permute-start.9
  74.1 9.0 %collective-permute-done.10 = bf16[256,256]{0,1:T(8,128)(2,1)S(1)} collective-permute-done((bf16[256,256]{0,1:T(8,128)(2,1)S(1)}, bf16[256,256]{0,1:T(8,128)(2,1)S(1)}, u32[]{:S(2)}, u32[]{:S(2)}) %collective-permute-start.10) | collective-permute-done | bytes 131104 | tf_op jit(solution)/shard_map/ppermute | solution.py:21
  84.6 3.6 %fusion.55 = f32[768,2048]{1,0:T(8,128)} fusion(bf16[256,2048]{1,0:T(8,128)(2,1)S(1)} %copy-done, f32[256,512]{0,1:T(8,128)S(1)} %bitcast.58, f32[256,128]{0,1:T(8,128)S(1)} %add_add_fusion.1, f32[256,128]{0,1:T(8,128)S(1)} %get-tuple-element.12), kind=kOutput, calls=%fused_computation.103 | convolution fusion | flops 805896192 | bytes 8126464 | tf_op jit(solution)/shard_map/rc,rd->cd/dot_general | solution.py:143
  88.3 4.0 %fusion.8 = bf16[256,2048]{1,0:T(8,128)(2,1)} fusion(bf16[1,1536,2048]{2,1,0:T(8,128)(2,1)} %copy-done.2, s32[]{:T(128)S(6)} %select_n.22, f32[256,512]{0,1:T(8,128)S(1)} %bitcast.59, f32[256,128]{0,1:T(8,128)S(1)} %add_add_fusion.1, f32[256,128]{0,1:T(8,128)S(1)} %get-tuple-element.12), kind=kOutput, calls=%fused_computation.10 | convolution fusion | flops 806420480 | bytes 4980740 | tf_op jit(solution)/shard_map/dot_general | solution.py:137
  92.3 60.8 %reduce-scatter.5.cloned.1.call-done = f32[96,2048]{1,0:T(8,128)} async-done(((f32[768,2048]{1,0:T(8,128)}), f32[96,2048]{1,0:T(8,128)}) %reduce-scatter.5.cloned.1.call-update) | async-done | bytes 786448 | tf_op jit(solution)/shard_map/reduce_scatter | solution.py:142
  153.2 1.2 convert_element_type.61
  154.3 1.5 collective-permute-start.11
  156.7 11.1 %collective-permute-done.11 = bf16[96,2048]{1,0:T(8,128)(2,1)S(1)} collective-permute-done((bf16[96,2048]{1,0:T(8,128)(2,1)S(1)}, bf16[96,2048]{1,0:T(8,128)(2,1)S(1)}, u32[]{:S(2)}, u32[]{:S(2)}) %collective-permute-start.11) | collective-permute-done | bytes 393248 | tf_op jit(solution)/shard_map/ppermute | solution.py:25
  167.8 2.2 %fusion.34 = f32[1,96,2048]{2,1,0:T(8,128)} fusion(f32[96,2048]{1,0:T(8,128)} %reduce-scatter.5.cloned.1.call-done, bf16[96,2048]{1,0:T(8,128)(2,1)S(1)} %collective-permute-done.11, pred[96]{0:T(512)(128)(4,1)S(1)} %add_compare_fusion), kind=kLoop, calls=%fused_computation.30 | loop fusion | flops 589824 | bytes 1966176 | tf_op jit(solution)/shard_map/broadcast_in_dim | solution.py:152
  170.0 14.2 %reduce-scatter.3.cloned.1.call-done = bf16[256,512]{1,0:T(8,128)(2,1)} async-done(((bf16[256,2048]{1,0:T(8,128)(2,1)}), bf16[256,512]{1,0:T(8,128)(2,1)}) %reduce-scatter.3.cloned.1.call-update) | async-done | bytes 262160 | tf_op jit(solution)/shard_map/reduce_scatter | solution.py:138
  (69 shorter events, 7.2 us)
Async XLA Ops:
  7.2 47.7 %copy-start = (bf16[256,2048]{1,0:T(8,128)(2,1)S(1)}, bf16[256,2048]{1,0:T(8,128)(2,1)}, u32[]{:S(2)}) copy-start(bf16[256,2048]{1,0:T(8,128)(2,1)} %param.6) | copy-start | bytes 3145732
  7.2 46.5 %copy-start.1 = (bf16[1,96,2048]{2,1,0:T(8,128)(2,1)S(1)}, bf16[1,96,2048]{2,1,0:T(8,128)(2,1)}, u32[]{:S(2)}) copy-start(bf16[1,96,2048]{2,1,0:T(8,128)(2,1)} %param.7) | copy-start | bytes 1179652
  7.2 146.0 %reduce-scatter.5.cloned.1.call-start = ((), (), s32[]{:S(2)}) async-start(), calls=%async_computation.3 | async-start | bytes 7077888 | tf_op jit(solution)/shard_map/reduce_scatter | solution.py:142
  7.2 9.1 %collective-permute-start = (bf16[1,96,2048]{2,1,0:T(8,128)(2,1)}, bf16[1,96,2048]{2,1,0:T(8,128)(2,1)S(1)}, u32[]{:S(2)}, u32[]{:S(2)}) collective-permute-start(bf16[1,96,2048]{2,1,0:T(8,128)(2,1)} %param.7), channel_id=1, source_target_pairs={{0,4},{4,8},{8,12},{12,16},{16,20},{20,24},{24,28},{28,0},{1,5},{5... | collective-permute-start | bytes 1179656 | tf_op jit(solution)/shard_map/ppermute | solution.py:106
  16.3 10.4 %collective-permute-start.1 = (bf16[1,96,2048]{2,1,0:T(8,128)(2,1)S(1)}, bf16[1,96,2048]{2,1,0:T(8,128)(2,1)S(1)}, u32[]{:S(2)}, u32[]{:S(2)}) collective-permute-start(bf16[1,96,2048]{2,1,0:T(8,128)(2,1)S(1)} %collective-permute-done), channel_id=1, source_target_pairs={{0,4},{4,8},{8,12},{12,16},{16,20},{20,24},{24,28},{28,0},{1,5},{5... | collective-permute-start | bytes 1179656 | tf_op jit(solution)/shard_map/ppermute | solution.py:106
  16.3 10.5 %collective-permute-start.4 = (bf16[1,96,2048]{2,1,0:T(8,128)(2,1)}, bf16[1,96,2048]{2,1,0:T(8,128)(2,1)S(1)}, u32[]{:S(2)}, u32[]{:S(2)}) collective-permute-start(bf16[1,96,2048]{2,1,0:T(8,128)(2,1)} %param.7), channel_id=1, source_target_pairs={{0,28},{4,0},{8,4},{12,8},{16,12},{20,16},{24,20},{28,24},{1,29},{... | collective-permute-start | bytes 1179656 | tf_op jit(solution)/shard_map/ppermute | solution.py:109
  26.7 11.0 %collective-permute-start.2 = (bf16[1,96,2048]{2,1,0:T(8,128)(2,1)S(1)}, bf16[1,96,2048]{2,1,0:T(8,128)(2,1)S(1)}, u32[]{:S(2)}, u32[]{:S(2)}) collective-permute-start(bf16[1,96,2048]{2,1,0:T(8,128)(2,1)S(1)} %collective-permute-done.1), channel_id=1, source_target_pairs={{0,4},{4,8},{8,12},{12,16},{16,20},{20,24},{24,28},{28,0},{1,5},{5... | collective-permute-start | bytes 1179656 | tf_op jit(solution)/shard_map/ppermute | solution.py:106
  26.8 12.9 %collective-permute-start.5 = (bf16[1,96,2048]{2,1,0:T(8,128)(2,1)S(1)}, bf16[1,96,2048]{2,1,0:T(8,128)(2,1)}, u32[]{:S(2)}, u32[]{:S(2)}) collective-permute-start(bf16[1,96,2048]{2,1,0:T(8,128)(2,1)S(1)} %collective-permute-done.4), channel_id=1, source_target_pairs={{0,28},{4,0},{8,4},{12,8},{16,12},{20,16},{24,20},{28,24},{1,29},{... | collective-permute-start | bytes 1179656 | tf_op jit(solution)/shard_map/ppermute | solution.py:109
  37.7 11.5 %collective-permute-start.3 = (bf16[1,96,2048]{2,1,0:T(8,128)(2,1)S(1)}, bf16[1,96,2048]{2,1,0:T(8,128)(2,1)}, u32[]{:S(2)}, u32[]{:S(2)}) collective-permute-start(bf16[1,96,2048]{2,1,0:T(8,128)(2,1)S(1)} %collective-permute-done.2), channel_id=1, source_target_pairs={{0,4},{4,8},{8,12},{12,16},{16,20},{20,24},{24,28},{28,0},{1,5},{5... | collective-permute-start | bytes 1179656 | tf_op jit(solution)/shard_map/ppermute | solution.py:106
  39.8 12.7 %collective-permute-start.6 = (bf16[1,96,2048]{2,1,0:T(8,128)(2,1)}, bf16[1,96,2048]{2,1,0:T(8,128)(2,1)S(1)}, u32[]{:S(2)}, u32[]{:S(2)}) collective-permute-start(bf16[1,96,2048]{2,1,0:T(8,128)(2,1)} %collective-permute-done.5), channel_id=1, source_target_pairs={{0,28},{4,0},{8,4},{12,8},{16,12},{20,16},{24,20},{28,24},{1,29},{... | collective-permute-start | bytes 1179656 | tf_op jit(solution)/shard_map/ppermute | solution.py:109
  53.7 2.3 %copy-start.4 = (f32[128]{0:T(128)S(1)}, f32[128]{0:T(128)}, u32[]{:S(2)}) copy-start(f32[128]{0:T(128)} %param.9) | copy-start | bytes 1540
  54.8 10.1 %copy-start.3 = (f32[128]{0:T(128)S(1)}, f32[128]{0:T(128)}, u32[]{:S(2)}) copy-start(f32[128]{0:T(128)} %param.8) | copy-start | bytes 1540
  54.8 2.7 %copy-start.2 = (bf16[1,1536,2048]{2,1,0:T(8,128)(2,1)}, bf16[1,1536,2048]{2,1,0:T(8,128)(2,1)S(1)}, u32[]{:S(2)}) copy-start(bf16[1,1536,2048]{2,1,0:T(8,128)(2,1)S(1)} %constant_dynamic-update-slice_fusion) | copy-start | bytes 18874372
  58.0 7.2 %collective-permute-start.7 = (bf16[256,256]{0,1:T(8,128)(2,1)S(1)}, bf16[256,256]{0,1:T(8,128)(2,1)S(1)}, u32[]{:S(2)}, u32[]{:S(2)}) collective-permute-start(bf16[256,256]{0,1:T(8,128)(2,1)S(1)} %pad_maximum_fusion.2), channel_id=1, source_target_pairs={{0,8},{4,12},{8,16},{12,20},{16,24},{20,28},{1,9},{5,13},{9,17},{1... | collective-permute-start | bytes 393224 | tf_op jit(solution)/shard_map/ppermute | solution.py:21
  59.5 6.2 %collective-permute-start.8 = (bf16[256,256]{0,1:T(8,128)(2,1)S(1)}, bf16[256,256]{0,1:T(8,128)(2,1)S(1)}, u32[]{:S(2)}, u32[]{:S(2)}) collective-permute-start(bf16[256,256]{0,1:T(8,128)(2,1)S(1)} %pad_maximum_fusion.2), channel_id=1, source_target_pairs={{0,4},{4,8},{8,12},{12,16},{16,20},{20,24},{24,28},{1,5},{5,9},{9,... | collective-permute-start | bytes 393224 | tf_op jit(solution)/shard_map/ppermute | solution.py:21
  71.1 12.0 %collective-permute-start.10 = (bf16[256,256]{0,1:T(8,128)(2,1)S(1)}, bf16[256,256]{0,1:T(8,128)(2,1)S(1)}, u32[]{:S(2)}, u32[]{:S(2)}) collective-permute-start(bf16[256,256]{0,1:T(8,128)(2,1)S(1)} %get-tuple-element.11), channel_id=1, source_target_pairs={{8,0},{12,4},{16,8},{20,12},{24,16},{28,20},{9,1},{13,5},{17,9},{2... | collective-permute-start | bytes 393224 | tf_op jit(solution)/shard_map/ppermute | solution.py:21
  72.4 10.7 %collective-permute-start.9 = (bf16[256,256]{0,1:T(8,128)(2,1)S(1)}, bf16[256,256]{0,1:T(8,128)(2,1)S(1)}, u32[]{:S(2)}, u32[]{:S(2)}) collective-permute-start(bf16[256,256]{0,1:T(8,128)(2,1)S(1)} %get-tuple-element.10), channel_id=1, source_target_pairs={{4,0},{8,4},{12,8},{16,12},{20,16},{24,20},{28,24},{5,1},{9,5},{13... | collective-permute-start | bytes 393224 | tf_op jit(solution)/shard_map/ppermute | solution.py:21
  88.2 96.0 %reduce-scatter.3.cloned.1.call-start = ((), (), s32[]{:S(2)}) async-start(), calls=%async_computation.2 | async-start | bytes 1310720 | tf_op jit(solution)/shard_map/reduce_scatter | solution.py:138
  154.3 13.5 %collective-permute-start.11 = (bf16[96,2048]{1,0:T(8,128)(2,1)S(1)}, bf16[96,2048]{1,0:T(8,128)(2,1)S(1)}, u32[]{:S(2)}, u32[]{:S(2)}) collective-permute-start(bf16[96,2048]{1,0:T(8,128)(2,1)S(1)} %convert_element_type.61), channel_id=1, source_target_pairs={{0,1},{1,0},{2,3},{3,2},{4,5},{5,4},{6,7},{7,6},{8,9},{9,8},{10,11... | collective-permute-start | bytes 1179656 | tf_op jit(solution)/shard_map/ppermute | solution.py:25
Sparse Core Ops, SparseCore 0:
  88.4 64.7 reduce-scatter.4
  156.0 28.1 reduce-scatter.2
